TPU v7x, 256 devices: a whole 4x4x8 slice. The times are simulated.
256 devices in a mesh: slab: 64 (over z, y, core), quad: 4 (over x).
Axes of the slice: x: 4, y: 4, z: 8, core: 2. Of those that a mesh axis runs over, the one named last changes fastest.
Arguments:
- grain_cell: int32 [4, 2097152], P(None, ('slab', 'quad')), may hold values from 0 to 254, as said below
- grain_count: int32 [256], P(('slab', 'quad')), may hold values from 2048 to 8192, as said below
- grain_weight: float32 [2097152], P(('slab', 'quad')), may hold values from 0.05 to 0.95
- grain_volume: float32 [2097152], P(('slab', 'quad')), may hold values from 0.02 to 0.4
- grain_velocity: float32 [3, 2097152], P(None, ('slab', 'quad')), may hold values from -6 to 6
Outputs:
- pressure: float32 [256, 64, 256], P('slab', 'quad')
- drag: float32 [3, 2097152], P(None, ('slab', 'quad'))
Inputs may be any that keep to these rules, and one draw needn't show every extreme that they name: grain_cell[0] < 4, grain_cell[1] < 4, grain_cell[2] < 16, grain_cell[3] <= 254; among the slots of one device at most 4096 name the same quarter, and on every device exactly 4096 name one quarter. `grain_count`: some device has all 8192 slots occupied.
All inputs are finite; a program needn't handle non-finite values.
Results may differ from a plain program's by a relative error of at most 0.00002.
Values sent between devices are 32-bit elements; how exact they have to be, the bound alone decides.
A program may use at most 128 MiB of HBM per device.

v0:
```python
import jax
import jax.numpy as jnp
from jax import lax
from jax.sharding import PartitionSpec as P

CH = 4
CA = 16
CB = 256
ITERS = 12
damping = 0.05
source_gain = 4.0


def extended(block, sides, width):
    for axis, dim in sides:
        count = lax.axis_size(axis)
        forward = [(i, i + 1) for i in range(count - 1)]
        backward = [(target, source) for source, target in forward]
        low = lax.ppermute(
            lax.slice_in_dim(block, block.shape[dim] - width, None, axis=dim), axis, forward
        )
        high = lax.ppermute(lax.slice_in_dim(block, 0, width, axis=dim), axis, backward)
        block = jnp.concatenate([low, block, high], axis=dim)
    return block


def neighbours(padded):
    centre = padded[1:-1, 1:-1]
    along = jnp.pad(centre, ((0, 0), (0, 0), (1, 1)))
    total = padded[2:, 1:-1] + padded[:-2, 1:-1] + padded[1:-1, 2:] + padded[1:-1, :-2]
    return total + along[:, :, 2:] + along[:, :, :-2]


def gradient(wide):
    vel_height = -0.5 * (wide[2:, 1:-1, 1:-1] - wide[:-2, 1:-1, 1:-1])
    vel_across = -0.5 * (wide[1:-1, 2:, 1:-1] - wide[1:-1, :-2, 1:-1])
    vel_along = -0.5 * (wide[1:-1, 1:-1, 2:] - wide[1:-1, 1:-1, :-2])
    return (vel_height, vel_across, vel_along)


def body(grain_cell, grain_count, grain_weight, grain_volume, grain_velocity):
    quarters = lax.axis_size("quad")
    layers, across_cells, along_cells = (CH, CA, CB)
    block = layers * across_cells * along_cells
    slots = jnp.arange(grain_weight.shape[0], dtype=jnp.int32)
    valid = (slots < grain_count[0]).astype(jnp.float32)
    mass = valid * grain_volume
    upper = 1.0 - grain_weight
    target = (
        (grain_cell[0] * layers + grain_cell[1]) * across_cells + grain_cell[2]
    ) * along_cells + grain_cell[3]
    amounts = jnp.stack([mass, mass * grain_velocity[0]])
    partial_value = jnp.zeros((2, quarters * block), jnp.float32)
    partial_value = (
        partial_value.at[:, target]
        .add(amounts * grain_weight)
        .at[:, target + 1]
        .add(amounts * upper)
    )
    partial_value = partial_value.reshape(2, quarters * layers, across_cells, along_cells)
    field = lax.psum_scatter(partial_value, "quad", scatter_dimension=1, tiled=True)
    solid = field[0]
    voidage = 1.0 / (1.0 + solid)
    source = source_gain * field[1]
    start = jnp.zeros((layers, across_cells, along_cells), jnp.float32)

    def relax(repeat, pressure):
        padded = extended(pressure, (("slab", 0), ("quad", 1)), 1)
        return (source + voidage * neighbours(padded)) / (6.0 * voidage + damping)

    pressure = lax.fori_loop(0, ITERS, relax, start)
    rimmed_p = extended(pressure, (("slab", 0), ("quad", 1)), 1)
    vel_height, vel_across, vel_along = gradient(jnp.pad(rimmed_p, ((0, 0), (0, 0), (1, 1))))
    stacked = jnp.stack([vel_height, vel_across, vel_along, solid])
    table = lax.all_gather(stacked, "quad", axis=2, tiled=True)
    across_all = across_cells * quarters
    table = table.reshape(4, layers * across_all * along_cells)
    source_index = (
        grain_cell[1] * across_all + grain_cell[0] * across_cells + grain_cell[2]
    ) * along_cells + grain_cell[3]
    sampled = grain_weight * table[:, source_index] + upper * table[:, source_index + 1]
    factor = mass * (1.0 + sampled[3]) ** 2
    drag = factor * (sampled[:3] - grain_velocity)
    return (pressure, drag)


def solution(mesh):
    placed = (
        P(None, ("slab", "quad")),
        P(("slab", "quad")),
        P(("slab", "quad")),
        P(("slab", "quad")),
        P(None, ("slab", "quad")),
    )
    return jax.shard_map(
        body,
        mesh=mesh,
        in_specs=placed,
        out_specs=(P("slab", "quad", None), P(None, ("slab", "quad"))),
        check_vma=False,
    )
```

profile of v0, /device:TPU:8, one launch (start us, length us, event | category | flops | bytes accessed | tf_op | source)
XLA Modules:
  0.0 598.2 jit_solution(5532912857880428166)
XLA Ops:
  12.5 2.7 copy.19
  15.2 2.7 copy.20
  18.0 57.5 %scatter_custom_fusion = f32[2,65536]{0,1:T(8,128)} fusion(s32[8192]{0:T(1024)S(1)} %bitcast.61, f32[8192,2]{1,0:T(8,128)} %copy.19, f32[]{:T(128)} %constant.44.clone.1), kind=kCustom, calls=%fused_computation.26 | custom fusion | flops 16384 | bytes 524800 | tf_op jit(solution)/shard_map/scatter-add | solution.py:56
  75.5 61.4 %scatter_fusion = f32[2,65536]{0,1:T(8,128)} fusion(f32[2,65536]{0,1:T(8,128)} %scatter_custom_fusion, s32[8192]{0:T(1024)S(1)} %bitcast.58, f32[8192,2]{1,0:T(8,128)} %copy.20), kind=kCustom, calls=%fused_computation.3 | custom fusion | flops 16384 | bytes 229376 | tf_op jit(solution)/shard_map/scatter-add | solution.py:58
  136.9 20.1 %copy.21 = f32[2,16,16,256]{3,2,1,0:T(8,128)} copy(f32[2,16,16,256]{0,3,2,1:T(8,128)} %bitcast.51) | data formatting | bytes 1048576 | tf_op jit(solution)/shard_map/reshape | solution.py:60
  158.4 50.0 %all-reduce.5.cloned.1.call-done = f32[2,16,16,256]{3,2,1,0:T(8,128)} async-done(((f32[2,16,16,256]{3,2,1,0:T(8,128)}), f32[2,16,16,256]{3,2,1,0:T(8,128)}) %all-reduce.5.cloned.1.call-update) | async-done | bytes 524304
  209.3 178.4 %while.13 = (s32[]{:T(128)}, f32[4,16,256]{2,1,0:T(8,128)S(1)}, f32[4,16,256]{2,1,0:T(8,128)S(1)}, f32[4,16,256]{2,1,0:T(8,128)S(1)}, s32[]{:T(128)}, /*index=5*/s32[]{:T(128)}) while((s32[]{:T(128)}, f32[4,16,256]{2,1,0:T(8,128)S(1)}, f32[4,16,256]{2,1,0:T(8,128)S(1)}, f32[4,16,256]{2,1,0:T(8,128)S(1)}, s32[]{:T(128)}, ...), condition=%wide.region_4.5_spmd.clone, body=%wide.region_3.4_spmd.clone.sunk | while | flops 317443 | bytes 794863 | solution.py:71
  211.3 2.4 collective-permute-start.1
  213.7 2.6 collective-permute-done.1
  220.1 4.2 collective-permute-done.3
  226.4 2.4 collective-permute-start.1
  228.8 2.6 collective-permute-done.1
  231.4 3.6 collective-permute-start.2
  236.4 4.2 collective-permute-done.3
  242.6 2.4 collective-permute-start.1
  245.1 2.6 collective-permute-done.1
  247.7 2.9 collective-permute-start.2
  251.9 4.2 collective-permute-done.3
  260.6 2.6 collective-permute-done.1
  266.5 4.2 collective-permute-done.3
  275.2 2.6 collective-permute-done.1
  281.1 4.2 collective-permute-done.3
  289.8 2.6 collective-permute-done.1
  295.7 4.2 collective-permute-done.3
  304.4 2.6 collective-permute-done.1
  310.3 4.2 collective-permute-done.3
  319.0 2.6 collective-permute-done.1
  325.0 4.2 collective-permute-done.3
  333.7 2.6 collective-permute-done.1
  339.6 4.2 collective-permute-done.3
  348.3 2.6 collective-permute-done.1
  354.2 4.2 collective-permute-done.3
  362.9 2.6 collective-permute-done.1
  368.8 4.2 collective-permute-done.3
  375.1 3.9 collective-permute-start.1
  383.4 4.2 collective-permute-done.3
  387.7 6.0 collective-permute-start.5
  395.7 6.4 %collective-permute-done.4 = f32[1,16,256]{2,1,0:T(8,128)S(1)} collective-permute-done((f32[1,16,256]{2,1,0:T(8,128)S(1)}, f32[1,16,256]{2,1,0:T(8,128)S(1)}, u32[]{:S(2)}, u32[]{:S(2)}) %collective-permute-start.4) | collective-permute-done | bytes 16416 | tf_op jit(solution)/shard_map/ppermute | solution.py:22
  403.4 4.7 collective-permute-start.7
  410.4 62.0 %all-gather.2.cloned.1.call-done = f32[4,4,64,256]{3,2,1,0:T(8,128)} async-done(((f32[4,4,16,256]{3,2,1,0:T(8,128)}), f32[4,4,64,256]{3,2,1,0:T(8,128)}) %all-gather.2.cloned.1.call-update) | async-done | bytes 1048592 | tf_op jit(solution)/shard_map/all_gather | solution.py:75
  472.4 17.7 %copy.22 = f32[4,4,64,256]{0,3,2,1:T(8,128)} copy(f32[4,4,64,256]{3,2,1,0:T(8,128)} %all-gather.2.cloned.1.call-done) | data formatting | bytes 2097152 | tf_op jit(solution)/shard_map/all_gather | solution.py:75
  490.1 38.4 %gather_fusion = f32[8192,4]{1,0:T(8,128)} fusion(f32[4,65536]{0,1:T(8,128)} %bitcast.52, s32[8192]{0:T(1024)S(1)} %broadcast_clamp_fusion.1), kind=kCustom, calls=%fused_computation | custom fusion | bytes 294912 | tf_op jit(solution)/shard_map/gather | solution.py:81
  528.5 38.4 %gather_fusion.1 = f32[8192,4]{1,0:T(8,128)} fusion(f32[4,65536]{0,1:T(8,128)} %bitcast.53, s32[8192]{0:T(1024)S(1)} %broadcast_clamp_fusion), kind=kCustom, calls=%fused_computation.1 | custom fusion | bytes 294912 | tf_op jit(solution)/shard_map/gather | solution.py:81
  566.9 7.0 %add_bitcast_fusion = f32[4,8192]{0,1:T(8,128)S(1)} fusion(f32[8192,4]{1,0:T(8,128)} %gather_fusion.1, f32[8192,4]{1,0:T(8,128)} %gather_fusion, f32[8192]{0:T(1024)S(1)} %broadcast_subtract_fusion, f32[8192]{0:T(1024)S(1)} %copy-done.2), kind=kLoop, calls=%fused_computation.31 | loop fusion | flops 98304 | bytes 458752 | tf_op jit(solution)/shard_map/add | solution.py:81
  578.2 2.8 copy.23
  581.1 2.6 copy.24
  583.7 4.2 broadcast_multiply_fusion
  587.9 3.5 copy.25
  (157 shorter events, 96.6 us)
Async XLA Ops:
  7.2 201.2 %all-reduce.5.cloned.1.call-start = ((), (), s32[]{:S(2)}) async-start(), calls=%async_computation.1 | async-start | bytes 1048576
  157.1 315.3 %all-gather.2.cloned.1.call-start = ((), (), s32[]{:S(2)}) async-start(), calls=%async_computation | async-start | bytes 1310720 | tf_op jit(solution)/shard_map/all_gather | solution.py:75
  209.3 4.3 collective-permute-start
  211.3 5.1 collective-permute-start.1
  216.3 3.7 collective-permute-start.2
  218.8 5.5 collective-permute-start.3
  224.4 4.3 collective-permute-start
  226.4 5.1 collective-permute-start.1
  231.4 4.9 collective-permute-start.2
  235.0 5.5 collective-permute-start.3
  240.7 4.3 collective-permute-start
  242.6 5.1 collective-permute-start.1
  247.7 4.2 collective-permute-start.2
  250.6 5.5 collective-permute-start.3
  256.3 4.3 collective-permute-start
  258.2 5.1 collective-permute-start.1
  263.3 3.3 collective-permute-start.2
  265.2 5.5 collective-permute-start.3
  270.9 4.3 collective-permute-start
  272.8 5.1 collective-permute-start.1
  277.9 3.3 collective-permute-start.2
  279.8 5.5 collective-permute-start.3
  285.5 4.3 collective-permute-start
  287.4 5.1 collective-permute-start.1
  294.4 5.5 collective-permute-start.3
  300.1 4.3 collective-permute-start
  302.0 5.1 collective-permute-start.1
  307.1 3.3 collective-permute-start.2
  309.0 5.5 collective-permute-start.3
  314.7 4.3 collective-permute-start
  316.6 5.1 collective-permute-start.1
  323.6 5.5 collective-permute-start.3
  329.3 4.3 collective-permute-start
  331.2 5.1 collective-permute-start.1
  338.2 5.5 collective-permute-start.3
  343.9 4.3 collective-permute-start
  345.8 5.1 collective-permute-start.1
  352.8 5.6 collective-permute-start.3
  358.6 4.3 collective-permute-start
  360.5 5.1 collective-permute-start.1
  367.4 5.5 collective-permute-start.3
  373.1 5.8 collective-permute-start
  375.1 5.1 collective-permute-start.1
  382.1 5.5 collective-permute-start.3
  387.7 7.9 %collective-permute-start.5 = (f32[1,16,256]{2,1,0:T(8,128)S(1)}, f32[1,16,256]{2,1,0:T(8,128)S(1)}, u32[]{:S(2)}, u32[]{:S(2)}) collective-permute-start(f32[1,16,256]{2,1,0:T(8,128)S(1)} %get-tuple-element.105), channel_id=1, source_target_pairs={{0,4},{4,8},{8,12},{12,16},{16,20},{20,24},{24,28},{28,32},{32,36}... | collective-permute-start | bytes 49160 | tf_op jit(solution)/shard_map/ppermute | solution.py:19
  393.7 8.4 %collective-permute-start.4 = (f32[1,16,256]{2,1,0:T(8,128)S(1)}, f32[1,16,256]{2,1,0:T(8,128)S(1)}, u32[]{:S(2)}, u32[]{:S(2)}) collective-permute-start(f32[1,16,256]{2,1,0:T(8,128)S(1)} %get-tuple-element.104), channel_id=1, source_target_pairs={{4,0},{8,4},{12,8},{16,12},{20,16},{24,20},{28,24},{32,28},{36,32}... | collective-permute-start | bytes 49160 | tf_op jit(solution)/shard_map/ppermute | solution.py:22
  402.1 6.0 %collective-permute-start.6 = (f32[6,1,256]{2,1,0:T(1,128)S(1)}, f32[6,1,256]{2,1,0:T(1,128)S(1)}, u32[]{:S(2)}, u32[]{:S(2)}) collective-permute-start(f32[6,1,256]{2,1,0:T(1,128)S(1)} %get-tuple-element.101), channel_id=1, source_target_pairs={{1,0},{2,1},{3,2},{5,4},{6,5},{7,6},{9,8},{10,9},{11,10},{13,12},{... | collective-permute-start | bytes 18440 | tf_op jit(solution)/shard_map/ppermute | solution.py:22
  403.4 5.9 collective-permute-start.7
  (11 other events, 305.8 us)
Sparse Core Ops, SparseCore 0:
  157.2 51.1 all-reduce.4
  410.5 61.8 all-gather.1
where the time goes:
time: 601 us; the launch traced here: 598 us
  waiting for transfers between devices  200 us (33%)
  other arithmetic  140 us (23%)
  local copies, waits for them, and re-layouts  133 us (22%)
  starting transfers between devices  109 us (18%)
  between operations  15.6 us (3%)
    scatter-add x2, other arithmetic, body(): partial_value = partial_value.at[:, target].add(amounts * grain_weight).a...  119 us
    ppermute x26, starting transfers between devices, extended(): lax.ppermute(lax.slice_in_dim(block, block.shape[dim] - width, None, axis...  67.2 us
    all_gather x1, waiting for transfers between devices, body(): table = lax.all_gather(stacked, 'quad', axis=2, tiled=True)  62 us
    ppermute x26, waiting for transfers between devices, extended(): lax.ppermute(lax.slice_in_dim(block, 0, width, axis=dim), axis, backward)  56.8 us
    unnamed x3, waiting for transfers between devices  50 us
    ppermute x26, starting transfers between devices, extended(): lax.ppermute(lax.slice_in_dim(block, 0, width, axis=dim), axis, backward)  41.8 us
    gather x1, local copies, waits for them, and re-layouts, body(): table[:, source_index + 1]  38.4 us
    gather x1, local copies, waits for them, and re-layouts, body(): table[:, source_index]  38.4 us
  transfers between devices with their start and end apart: 54, of which 28 were waited for; matrix products, arithmetic and copies ran while one was open for 0% of the time, Pallas kernels for 0%

commit v1 on v0

--- a/solution.py
+++ b/solution.py
@@ -72,7 +72,9 @@
     rimmed_p = extended(pressure, (("slab", 0), ("quad", 1)), 1)
     vel_height, vel_across, vel_along = gradient(jnp.pad(rimmed_p, ((0, 0), (0, 0), (1, 1))))
     stacked = jnp.stack([vel_height, vel_across, vel_along, solid])
-    table = lax.all_gather(stacked, "quad", axis=2, tiled=True)
+    table = jnp.concatenate(
+        lax.all_to_all(jnp.stack([stacked] * lax.axis_size("quad")), "quad", 0, 0), axis=2
+    )
     across_all = across_cells * quarters
     table = table.reshape(4, layers * across_all * along_cells)
     source_index = (

time: 601 us -> 589 us (0.980)
  the two profiles are of different devices: /device:TPU:8 before, /device:TPU:121 now
where the time goes in v1:
time: 589 us; the launch traced here: 587 us
  starting transfers between devices  187 us (32%)
  other arithmetic  139 us (24%)
  local copies, waits for them, and re-layouts  132 us (22%)
  waiting for transfers between devices  112 us (19%)
  between operations  15.6 us (3%)
    ppermute x26, starting transfers between devices, extended(): lax.ppermute(lax.slice_in_dim(block, block.shape[dim] - width, None, axis...  137 us
    scatter-add x2, other arithmetic, body(): partial_value = partial_value.at[:, target].add(amounts * grain_weight).a...  119 us
    unnamed x2, waiting for transfers between devices  46.6 us
    ppermute x26, starting transfers between devices, extended(): lax.ppermute(lax.slice_in_dim(block, 0, width, axis=dim), axis, backward)  45.9 us
    ppermute x26, waiting for transfers between devices, extended(): lax.ppermute(lax.slice_in_dim(block, 0, width, axis=dim), axis, backward)  43.3 us
    gather x1, local copies, waits for them, and re-layouts, body(): table[:, source_index + 1]  38.3 us
    gather x1, local copies, waits for them, and re-layouts, body(): table[:, source_index]  38.3 us
    reshape x1, local copies, waits for them, and re-layouts, body(): partial_value.reshape(2, quarters * layers, across_cells, along_cells)  20.1 us
  transfers between devices with their start and end apart: 54, of which 28 were waited for; matrix products, arithmetic and copies ran while one was open for 0% of the time, Pallas kernels for 0%

profile of v1, /device:TPU:121, one launch (start us, length us, event | category | flops | bytes accessed | tf_op | source)
XLA Modules:
  0.0 586.9 jit_solution(3914998909556620562)
XLA Ops:
  12.5 2.7 copy.19
  15.2 2.7 copy.20
  18.0 57.5 %scatter_custom_fusion = f32[2,65536]{0,1:T(8,128)} fusion(s32[8192]{0:T(1024)S(1)} %bitcast.63, f32[8192,2]{1,0:T(8,128)} %copy.19, f32[]{:T(128)} %constant.44.clone.1), kind=kCustom, calls=%fused_computation.26 | custom fusion | flops 16384 | bytes 524800 | tf_op jit(solution)/shard_map/scatter-add | solution.py:56
  75.5 61.4 %scatter_fusion = f32[2,65536]{0,1:T(8,128)} fusion(f32[2,65536]{0,1:T(8,128)} %scatter_custom_fusion, s32[8192]{0:T(1024)S(1)} %bitcast.60, f32[8192,2]{1,0:T(8,128)} %copy.20), kind=kCustom, calls=%fused_computation.3 | custom fusion | flops 16384 | bytes 229376 | tf_op jit(solution)/shard_map/scatter-add | solution.py:58
  136.9 20.1 %copy.21 = f32[2,16,16,256]{3,2,1,0:T(8,128)} copy(f32[2,16,16,256]{0,3,2,1:T(8,128)} %bitcast.52) | data formatting | bytes 1048576 | tf_op jit(solution)/shard_map/reshape | solution.py:60
  158.4 46.6 %all-reduce.5.cloned.1.call-done = f32[2,16,16,256]{3,2,1,0:T(8,128)} async-done(((f32[2,16,16,256]{3,2,1,0:T(8,128)}), f32[2,16,16,256]{3,2,1,0:T(8,128)}) %all-reduce.5.cloned.1.call-update) | async-done | bytes 524304
  205.8 216.4 %while.13 = (s32[]{:T(128)}, f32[4,16,256]{2,1,0:T(8,128)S(1)}, f32[4,16,256]{2,1,0:T(8,128)S(1)}, f32[4,16,256]{2,1,0:T(8,128)S(1)}, s32[]{:T(128)}, /*index=5*/s32[]{:T(128)}) while((s32[]{:T(128)}, f32[4,16,256]{2,1,0:T(8,128)S(1)}, f32[4,16,256]{2,1,0:T(8,128)S(1)}, f32[4,16,256]{2,1,0:T(8,128)S(1)}, s32[]{:T(128)}, ...), condition=%wide.region_4.5_spmd.clone, body=%wide.region_3.4_spmd.clone.sunk | while | flops 317443 | bytes 794863 | solution.py:71
  205.9 4.8 collective-permute-start
  210.7 4.2 collective-permute-start.1
  219.2 3.1 collective-permute-done.3
  222.5 3.2 collective-permute-start
  225.7 7.6 %collective-permute-start.1 = (f32[1,16,256]{2,1,0:T(8,128)S(1)}, f32[1,16,256]{2,1,0:T(8,128)S(1)}, u32[]{:S(2)}, u32[]{:S(2)}) collective-permute-start(f32[1,16,256]{2,1,0:T(8,128)S(1)} %get-tuple-element.140), channel_id=1, source_target_pairs={{0,4},{4,8},{8,12},{12,16},{16,20},{20,24},{24,28},{28,32},{32,36}... | collective-permute-start | bytes 49160 | tf_op jit(solution)/shard_map/while/body/eval_jaxpr/ppermute | solution.py:19
  234.2 3.4 collective-permute-start.2
  238.9 3.1 collective-permute-done.3
  244.1 9.0 %collective-permute-start.1 = (f32[1,16,256]{2,1,0:T(8,128)S(1)}, f32[1,16,256]{2,1,0:T(8,128)S(1)}, u32[]{:S(2)}, u32[]{:S(2)}) collective-permute-start(f32[1,16,256]{2,1,0:T(8,128)S(1)} %get-tuple-element.140), channel_id=1, source_target_pairs={{0,4},{4,8},{8,12},{12,16},{16,20},{20,24},{24,28},{28,32},{32,36}... | collective-permute-start | bytes 49160 | tf_op jit(solution)/shard_map/while/body/eval_jaxpr/ppermute | solution.py:19
  253.9 2.4 collective-permute-start.2
  257.7 3.1 collective-permute-done.3
  262.8 9.0 %collective-permute-start.1 = (f32[1,16,256]{2,1,0:T(8,128)S(1)}, f32[1,16,256]{2,1,0:T(8,128)S(1)}, u32[]{:S(2)}, u32[]{:S(2)}) collective-permute-start(f32[1,16,256]{2,1,0:T(8,128)S(1)} %get-tuple-element.140), channel_id=1, source_target_pairs={{0,4},{4,8},{8,12},{12,16},{16,20},{20,24},{24,28},{28,32},{32,36}... | collective-permute-start | bytes 49160 | tf_op jit(solution)/shard_map/while/body/eval_jaxpr/ppermute | solution.py:19
  275.6 3.1 collective-permute-done.3
  280.7 9.0 %collective-permute-start.1 = (f32[1,16,256]{2,1,0:T(8,128)S(1)}, f32[1,16,256]{2,1,0:T(8,128)S(1)}, u32[]{:S(2)}, u32[]{:S(2)}) collective-permute-start(f32[1,16,256]{2,1,0:T(8,128)S(1)} %get-tuple-element.140), channel_id=1, source_target_pairs={{0,4},{4,8},{8,12},{12,16},{16,20},{20,24},{24,28},{28,32},{32,36}... | collective-permute-start | bytes 49160 | tf_op jit(solution)/shard_map/while/body/eval_jaxpr/ppermute | solution.py:19
  293.5 3.1 collective-permute-done.3
  298.7 9.0 %collective-permute-start.1 = (f32[1,16,256]{2,1,0:T(8,128)S(1)}, f32[1,16,256]{2,1,0:T(8,128)S(1)}, u32[]{:S(2)}, u32[]{:S(2)}) collective-permute-start(f32[1,16,256]{2,1,0:T(8,128)S(1)} %get-tuple-element.140), channel_id=1, source_target_pairs={{0,4},{4,8},{8,12},{12,16},{16,20},{20,24},{24,28},{28,32},{32,36}... | collective-permute-start | bytes 49160 | tf_op jit(solution)/shard_map/while/body/eval_jaxpr/ppermute | solution.py:19
  311.4 3.1 collective-permute-done.3
  316.6 9.0 %collective-permute-start.1 = (f32[1,16,256]{2,1,0:T(8,128)S(1)}, f32[1,16,256]{2,1,0:T(8,128)S(1)}, u32[]{:S(2)}, u32[]{:S(2)}) collective-permute-start(f32[1,16,256]{2,1,0:T(8,128)S(1)} %get-tuple-element.140), channel_id=1, source_target_pairs={{0,4},{4,8},{8,12},{12,16},{16,20},{20,24},{24,28},{28,32},{32,36}... | collective-permute-start | bytes 49160 | tf_op jit(solution)/shard_map/while/body/eval_jaxpr/ppermute | solution.py:19
  329.4 3.1 collective-permute-done.3
  334.5 9.0 %collective-permute-start.1 = (f32[1,16,256]{2,1,0:T(8,128)S(1)}, f32[1,16,256]{2,1,0:T(8,128)S(1)}, u32[]{:S(2)}, u32[]{:S(2)}) collective-permute-start(f32[1,16,256]{2,1,0:T(8,128)S(1)} %get-tuple-element.140), channel_id=1, source_target_pairs={{0,4},{4,8},{8,12},{12,16},{16,20},{20,24},{24,28},{28,32},{32,36}... | collective-permute-start | bytes 49160 | tf_op jit(solution)/shard_map/while/body/eval_jaxpr/ppermute | solution.py:19
  347.3 3.1 collective-permute-done.3
  352.4 9.0 %collective-permute-start.1 = (f32[1,16,256]{2,1,0:T(8,128)S(1)}, f32[1,16,256]{2,1,0:T(8,128)S(1)}, u32[]{:S(2)}, u32[]{:S(2)}) collective-permute-start(f32[1,16,256]{2,1,0:T(8,128)S(1)} %get-tuple-element.140), channel_id=1, source_target_pairs={{0,4},{4,8},{8,12},{12,16},{16,20},{20,24},{24,28},{28,32},{32,36}... | collective-permute-start | bytes 49160 | tf_op jit(solution)/shard_map/while/body/eval_jaxpr/ppermute | solution.py:19
  365.2 3.1 collective-permute-done.3
  370.4 9.0 %collective-permute-start.1 = (f32[1,16,256]{2,1,0:T(8,128)S(1)}, f32[1,16,256]{2,1,0:T(8,128)S(1)}, u32[]{:S(2)}, u32[]{:S(2)}) collective-permute-start(f32[1,16,256]{2,1,0:T(8,128)S(1)} %get-tuple-element.140), channel_id=1, source_target_pairs={{0,4},{4,8},{8,12},{12,16},{16,20},{20,24},{24,28},{28,32},{32,36}... | collective-permute-start | bytes 49160 | tf_op jit(solution)/shard_map/while/body/eval_jaxpr/ppermute | solution.py:19
  383.1 3.1 collective-permute-done.3
  388.3 9.0 %collective-permute-start.1 = (f32[1,16,256]{2,1,0:T(8,128)S(1)}, f32[1,16,256]{2,1,0:T(8,128)S(1)}, u32[]{:S(2)}, u32[]{:S(2)}) collective-permute-start(f32[1,16,256]{2,1,0:T(8,128)S(1)} %get-tuple-element.140), channel_id=1, source_target_pairs={{0,4},{4,8},{8,12},{12,16},{16,20},{20,24},{24,28},{28,32},{32,36}... | collective-permute-start | bytes 49160 | tf_op jit(solution)/shard_map/while/body/eval_jaxpr/ppermute | solution.py:19
  401.1 3.1 collective-permute-done.3
  406.2 9.0 %collective-permute-start.1 = (f32[1,16,256]{2,1,0:T(8,128)S(1)}, f32[1,16,256]{2,1,0:T(8,128)S(1)}, u32[]{:S(2)}, u32[]{:S(2)}) collective-permute-start(f32[1,16,256]{2,1,0:T(8,128)S(1)} %get-tuple-element.140), channel_id=1, source_target_pairs={{0,4},{4,8},{8,12},{12,16},{16,20},{20,24},{24,28},{28,32},{32,36}... | collective-permute-start | bytes 49160 | tf_op jit(solution)/shard_map/while/body/eval_jaxpr/ppermute | solution.py:19
  419.0 3.1 collective-permute-done.3
  422.2 9.0 %collective-permute-start.5 = (f32[1,16,256]{2,1,0:T(8,128)S(1)}, f32[1,16,256]{2,1,0:T(8,128)S(1)}, u32[]{:S(2)}, u32[]{:S(2)}) collective-permute-start(f32[1,16,256]{2,1,0:T(8,128)S(1)} %get-tuple-element.105), channel_id=1, source_target_pairs={{0,4},{4,8},{8,12},{12,16},{16,20},{20,24},{24,28},{28,32},{32,36}... | collective-permute-start | bytes 49160 | tf_op jit(solution)/shard_map/ppermute | solution.py:19
  433.1 6.4 %collective-permute-done.4 = f32[1,16,256]{2,1,0:T(8,128)S(1)} collective-permute-done((f32[1,16,256]{2,1,0:T(8,128)S(1)}, f32[1,16,256]{2,1,0:T(8,128)S(1)}, u32[]{:S(2)}, u32[]{:S(2)}) %collective-permute-start.4) | collective-permute-done | bytes 16416 | tf_op jit(solution)/shard_map/ppermute | solution.py:22
  440.9 4.0 collective-permute-start.7
  447.1 3.7 all-to-all-start
  450.8 11.5 %all-to-all-done = f32[4,4,4,16,256]{4,3,2,1,0:T(8,128)S(1)} async-done(((f32[4,4,4,16,256]{4,3,2,1,0:T(8,128)}), f32[4,4,4,16,256]{4,3,2,1,0:T(8,128)S(1)}, u32[]{:S(2)}, u32[]{:S(2)}) %all-to-all-start) | async-done | bytes 1048608 | tf_op jit(solution)/shard_map/all_to_all | solution.py:76
  462.4 16.6 %copy.22 = f32[4,4,4,16,256]{0,4,3,2,1:T(8,128)} copy(f32[4,4,4,16,256]{4,3,1,0,2:T(8,128)S(1)} %bitcast.56) | data formatting | bytes 2097152 | tf_op jit(solution)/shard_map/reshape | solution.py:75
  479.0 38.3 %gather_fusion = f32[8192,4]{1,0:T(8,128)} fusion(f32[4,65536]{0,1:T(8,128)} %bitcast.53, s32[8192]{0:T(1024)S(1)} %broadcast_clamp_fusion.1), kind=kCustom, calls=%fused_computation | custom fusion | bytes 294912 | tf_op jit(solution)/shard_map/gather | solution.py:83
  517.3 38.3 %gather_fusion.1 = f32[8192,4]{1,0:T(8,128)} fusion(f32[4,65536]{0,1:T(8,128)} %bitcast.54, s32[8192]{0:T(1024)S(1)} %broadcast_clamp_fusion), kind=kCustom, calls=%fused_computation.1 | custom fusion | bytes 294912 | tf_op jit(solution)/shard_map/gather | solution.py:83
  555.6 7.0 %add_bitcast_fusion = f32[4,8192]{0,1:T(8,128)S(1)} fusion(f32[8192,4]{1,0:T(8,128)} %gather_fusion.1, f32[8192,4]{1,0:T(8,128)} %gather_fusion, f32[8192]{0:T(1024)S(1)} %broadcast_subtract_fusion, f32[8192]{0:T(1024)S(1)} %copy-done.2), kind=kLoop, calls=%fused_computation.31 | loop fusion | flops 98304 | bytes 458752 | tf_op jit(solution)/shard_map/add | solution.py:83
  566.8 2.8 copy.23
  569.7 2.7 copy.24
  572.4 4.2 broadcast_multiply_fusion
  576.6 3.5 copy.25
  (157 shorter events, 79.3 us)
Async XLA Ops:
  7.2 197.8 %all-reduce.5.cloned.1.call-start = ((), (), s32[]{:S(2)}) async-start(), calls=%async_computation.1 | async-start | bytes 1048576
  205.9 9.0 %collective-permute-start = (f32[1,16,256]{2,1,0:T(8,128)S(1)}, f32[1,16,256]{2,1,0:T(8,128)S(1)}, u32[]{:S(2)}, u32[]{:S(2)}) collective-permute-start(f32[1,16,256]{2,1,0:T(8,128)S(1)} %get-tuple-element.139), channel_id=1, source_target_pairs={{4,0},{8,4},{12,8},{16,12},{20,16},{24,20},{28,24},{32,28},{36,32}... | collective-permute-start | bytes 49160 | tf_op jit(solution)/shard_map/while/body/eval_jaxpr/ppermute | solution.py:22
  210.7 5.1 collective-permute-start.1
  215.7 3.5 collective-permute-start.2
  217.9 4.4 collective-permute-start.3
  222.5 10.9 %collective-permute-start = (f32[1,16,256]{2,1,0:T(8,128)S(1)}, f32[1,16,256]{2,1,0:T(8,128)S(1)}, u32[]{:S(2)}, u32[]{:S(2)}) collective-permute-start(f32[1,16,256]{2,1,0:T(8,128)S(1)} %get-tuple-element.139), channel_id=1, source_target_pairs={{4,0},{8,4},{12,8},{16,12},{20,16},{24,20},{28,24},{32,28},{36,32}... | collective-permute-start | bytes 49160 | tf_op jit(solution)/shard_map/while/body/eval_jaxpr/ppermute | solution.py:22
  225.7 8.5 %collective-permute-start.1 = (f32[1,16,256]{2,1,0:T(8,128)S(1)}, f32[1,16,256]{2,1,0:T(8,128)S(1)}, u32[]{:S(2)}, u32[]{:S(2)}) collective-permute-start(f32[1,16,256]{2,1,0:T(8,128)S(1)} %get-tuple-element.140), channel_id=1, source_target_pairs={{0,4},{4,8},{8,12},{12,16},{16,20},{20,24},{24,28},{28,32},{32,36}... | collective-permute-start | bytes 49160 | tf_op jit(solution)/shard_map/while/body/eval_jaxpr/ppermute | solution.py:19
  234.2 4.7 collective-permute-start.2
  237.6 4.4 collective-permute-start.3
  242.1 10.9 %collective-permute-start = (f32[1,16,256]{2,1,0:T(8,128)S(1)}, f32[1,16,256]{2,1,0:T(8,128)S(1)}, u32[]{:S(2)}, u32[]{:S(2)}) collective-permute-start(f32[1,16,256]{2,1,0:T(8,128)S(1)} %get-tuple-element.139), channel_id=1, source_target_pairs={{4,0},{8,4},{12,8},{16,12},{20,16},{24,20},{28,24},{32,28},{36,32}... | collective-permute-start | bytes 49160 | tf_op jit(solution)/shard_map/while/body/eval_jaxpr/ppermute | solution.py:22
  244.1 9.8 %collective-permute-start.1 = (f32[1,16,256]{2,1,0:T(8,128)S(1)}, f32[1,16,256]{2,1,0:T(8,128)S(1)}, u32[]{:S(2)}, u32[]{:S(2)}) collective-permute-start(f32[1,16,256]{2,1,0:T(8,128)S(1)} %get-tuple-element.140), channel_id=1, source_target_pairs={{0,4},{4,8},{8,12},{12,16},{16,20},{20,24},{24,28},{28,32},{32,36}... | collective-permute-start | bytes 49160 | tf_op jit(solution)/shard_map/while/body/eval_jaxpr/ppermute | solution.py:19
  253.9 3.8 collective-permute-start.2
  256.3 4.4 collective-permute-start.3
  260.9 10.9 %collective-permute-start = (f32[1,16,256]{2,1,0:T(8,128)S(1)}, f32[1,16,256]{2,1,0:T(8,128)S(1)}, u32[]{:S(2)}, u32[]{:S(2)}) collective-permute-start(f32[1,16,256]{2,1,0:T(8,128)S(1)} %get-tuple-element.139), channel_id=1, source_target_pairs={{4,0},{8,4},{12,8},{16,12},{20,16},{24,20},{28,24},{32,28},{36,32}... | collective-permute-start | bytes 49160 | tf_op jit(solution)/shard_map/while/body/eval_jaxpr/ppermute | solution.py:22
  262.8 9.8 %collective-permute-start.1 = (f32[1,16,256]{2,1,0:T(8,128)S(1)}, f32[1,16,256]{2,1,0:T(8,128)S(1)}, u32[]{:S(2)}, u32[]{:S(2)}) collective-permute-start(f32[1,16,256]{2,1,0:T(8,128)S(1)} %get-tuple-element.140), channel_id=1, source_target_pairs={{0,4},{4,8},{8,12},{12,16},{16,20},{20,24},{24,28},{28,32},{32,36}... | collective-permute-start | bytes 49160 | tf_op jit(solution)/shard_map/while/body/eval_jaxpr/ppermute | solution.py:19
  272.6 3.0 collective-permute-start.2
  274.3 4.4 collective-permute-start.3
  278.8 10.9 %collective-permute-start = (f32[1,16,256]{2,1,0:T(8,128)S(1)}, f32[1,16,256]{2,1,0:T(8,128)S(1)}, u32[]{:S(2)}, u32[]{:S(2)}) collective-permute-start(f32[1,16,256]{2,1,0:T(8,128)S(1)} %get-tuple-element.139), channel_id=1, source_target_pairs={{4,0},{8,4},{12,8},{16,12},{20,16},{24,20},{28,24},{32,28},{36,32}... | collective-permute-start | bytes 49160 | tf_op jit(solution)/shard_map/while/body/eval_jaxpr/ppermute | solution.py:22
  280.7 9.8 %collective-permute-start.1 = (f32[1,16,256]{2,1,0:T(8,128)S(1)}, f32[1,16,256]{2,1,0:T(8,128)S(1)}, u32[]{:S(2)}, u32[]{:S(2)}) collective-permute-start(f32[1,16,256]{2,1,0:T(8,128)S(1)} %get-tuple-element.140), channel_id=1, source_target_pairs={{0,4},{4,8},{8,12},{12,16},{16,20},{20,24},{24,28},{28,32},{32,36}... | collective-permute-start | bytes 49160 | tf_op jit(solution)/shard_map/while/body/eval_jaxpr/ppermute | solution.py:19
  292.2 4.4 collective-permute-start.3
  296.7 10.9 %collective-permute-start = (f32[1,16,256]{2,1,0:T(8,128)S(1)}, f32[1,16,256]{2,1,0:T(8,128)S(1)}, u32[]{:S(2)}, u32[]{:S(2)}) collective-permute-start(f32[1,16,256]{2,1,0:T(8,128)S(1)} %get-tuple-element.139), channel_id=1, source_target_pairs={{4,0},{8,4},{12,8},{16,12},{20,16},{24,20},{28,24},{32,28},{36,32}... | collective-permute-start | bytes 49160 | tf_op jit(solution)/shard_map/while/body/eval_jaxpr/ppermute | solution.py:22
  298.7 9.8 %collective-permute-start.1 = (f32[1,16,256]{2,1,0:T(8,128)S(1)}, f32[1,16,256]{2,1,0:T(8,128)S(1)}, u32[]{:S(2)}, u32[]{:S(2)}) collective-permute-start(f32[1,16,256]{2,1,0:T(8,128)S(1)} %get-tuple-element.140), channel_id=1, source_target_pairs={{0,4},{4,8},{8,12},{12,16},{16,20},{20,24},{24,28},{28,32},{32,36}... | collective-permute-start | bytes 49160 | tf_op jit(solution)/shard_map/while/body/eval_jaxpr/ppermute | solution.py:19
  310.1 4.4 collective-permute-start.3
  314.7 10.9 %collective-permute-start = (f32[1,16,256]{2,1,0:T(8,128)S(1)}, f32[1,16,256]{2,1,0:T(8,128)S(1)}, u32[]{:S(2)}, u32[]{:S(2)}) collective-permute-start(f32[1,16,256]{2,1,0:T(8,128)S(1)} %get-tuple-element.139), channel_id=1, source_target_pairs={{4,0},{8,4},{12,8},{16,12},{20,16},{24,20},{28,24},{32,28},{36,32}... | collective-permute-start | bytes 49160 | tf_op jit(solution)/shard_map/while/body/eval_jaxpr/ppermute | solution.py:22
  316.6 9.8 %collective-permute-start.1 = (f32[1,16,256]{2,1,0:T(8,128)S(1)}, f32[1,16,256]{2,1,0:T(8,128)S(1)}, u32[]{:S(2)}, u32[]{:S(2)}) collective-permute-start(f32[1,16,256]{2,1,0:T(8,128)S(1)} %get-tuple-element.140), channel_id=1, source_target_pairs={{0,4},{4,8},{8,12},{12,16},{16,20},{20,24},{24,28},{28,32},{32,36}... | collective-permute-start | bytes 49160 | tf_op jit(solution)/shard_map/while/body/eval_jaxpr/ppermute | solution.py:19
  326.4 3.0 collective-permute-start.2
  328.1 4.4 collective-permute-start.3
  332.6 10.9 %collective-permute-start = (f32[1,16,256]{2,1,0:T(8,128)S(1)}, f32[1,16,256]{2,1,0:T(8,128)S(1)}, u32[]{:S(2)}, u32[]{:S(2)}) collective-permute-start(f32[1,16,256]{2,1,0:T(8,128)S(1)} %get-tuple-element.139), channel_id=1, source_target_pairs={{4,0},{8,4},{12,8},{16,12},{20,16},{24,20},{28,24},{32,28},{36,32}... | collective-permute-start | bytes 49160 | tf_op jit(solution)/shard_map/while/body/eval_jaxpr/ppermute | solution.py:22
  334.5 9.8 %collective-permute-start.1 = (f32[1,16,256]{2,1,0:T(8,128)S(1)}, f32[1,16,256]{2,1,0:T(8,128)S(1)}, u32[]{:S(2)}, u32[]{:S(2)}) collective-permute-start(f32[1,16,256]{2,1,0:T(8,128)S(1)} %get-tuple-element.140), channel_id=1, source_target_pairs={{0,4},{4,8},{8,12},{12,16},{16,20},{20,24},{24,28},{28,32},{32,36}... | collective-permute-start | bytes 49160 | tf_op jit(solution)/shard_map/while/body/eval_jaxpr/ppermute | solution.py:19
  344.3 3.0 collective-permute-start.2
  346.0 4.4 collective-permute-start.3
  350.5 10.9 %collective-permute-start = (f32[1,16,256]{2,1,0:T(8,128)S(1)}, f32[1,16,256]{2,1,0:T(8,128)S(1)}, u32[]{:S(2)}, u32[]{:S(2)}) collective-permute-start(f32[1,16,256]{2,1,0:T(8,128)S(1)} %get-tuple-element.139), channel_id=1, source_target_pairs={{4,0},{8,4},{12,8},{16,12},{20,16},{24,20},{28,24},{32,28},{36,32}... | collective-permute-start | bytes 49160 | tf_op jit(solution)/shard_map/while/body/eval_jaxpr/ppermute | solution.py:22
  352.4 9.8 %collective-permute-start.1 = (f32[1,16,256]{2,1,0:T(8,128)S(1)}, f32[1,16,256]{2,1,0:T(8,128)S(1)}, u32[]{:S(2)}, u32[]{:S(2)}) collective-permute-start(f32[1,16,256]{2,1,0:T(8,128)S(1)} %get-tuple-element.140), channel_id=1, source_target_pairs={{0,4},{4,8},{8,12},{12,16},{16,20},{20,24},{24,28},{28,32},{32,36}... | collective-permute-start | bytes 49160 | tf_op jit(solution)/shard_map/while/body/eval_jaxpr/ppermute | solution.py:19
  363.9 4.4 collective-permute-start.3
  368.4 10.9 %collective-permute-start = (f32[1,16,256]{2,1,0:T(8,128)S(1)}, f32[1,16,256]{2,1,0:T(8,128)S(1)}, u32[]{:S(2)}, u32[]{:S(2)}) collective-permute-start(f32[1,16,256]{2,1,0:T(8,128)S(1)} %get-tuple-element.139), channel_id=1, source_target_pairs={{4,0},{8,4},{12,8},{16,12},{20,16},{24,20},{28,24},{32,28},{36,32}... | collective-permute-start | bytes 49160 | tf_op jit(solution)/shard_map/while/body/eval_jaxpr/ppermute | solution.py:22
  370.4 9.8 %collective-permute-start.1 = (f32[1,16,256]{2,1,0:T(8,128)S(1)}, f32[1,16,256]{2,1,0:T(8,128)S(1)}, u32[]{:S(2)}, u32[]{:S(2)}) collective-permute-start(f32[1,16,256]{2,1,0:T(8,128)S(1)} %get-tuple-element.140), channel_id=1, source_target_pairs={{0,4},{4,8},{8,12},{12,16},{16,20},{20,24},{24,28},{28,32},{32,36}... | collective-permute-start | bytes 49160 | tf_op jit(solution)/shard_map/while/body/eval_jaxpr/ppermute | solution.py:19
  381.8 4.4 collective-permute-start.3
  386.4 10.9 %collective-permute-start = (f32[1,16,256]{2,1,0:T(8,128)S(1)}, f32[1,16,256]{2,1,0:T(8,128)S(1)}, u32[]{:S(2)}, u32[]{:S(2)}) collective-permute-start(f32[1,16,256]{2,1,0:T(8,128)S(1)} %get-tuple-element.139), channel_id=1, source_target_pairs={{4,0},{8,4},{12,8},{16,12},{20,16},{24,20},{28,24},{32,28},{36,32}... | collective-permute-start | bytes 49160 | tf_op jit(solution)/shard_map/while/body/eval_jaxpr/ppermute | solution.py:22
  388.3 9.8 %collective-permute-start.1 = (f32[1,16,256]{2,1,0:T(8,128)S(1)}, f32[1,16,256]{2,1,0:T(8,128)S(1)}, u32[]{:S(2)}, u32[]{:S(2)}) collective-permute-start(f32[1,16,256]{2,1,0:T(8,128)S(1)} %get-tuple-element.140), channel_id=1, source_target_pairs={{0,4},{4,8},{8,12},{12,16},{16,20},{20,24},{24,28},{28,32},{32,36}... | collective-permute-start | bytes 49160 | tf_op jit(solution)/shard_map/while/body/eval_jaxpr/ppermute | solution.py:19
  399.8 4.4 collective-permute-start.3
  404.3 10.9 %collective-permute-start = (f32[1,16,256]{2,1,0:T(8,128)S(1)}, f32[1,16,256]{2,1,0:T(8,128)S(1)}, u32[]{:S(2)}, u32[]{:S(2)}) collective-permute-start(f32[1,16,256]{2,1,0:T(8,128)S(1)} %get-tuple-element.139), channel_id=1, source_target_pairs={{4,0},{8,4},{12,8},{16,12},{20,16},{24,20},{28,24},{32,28},{36,32}... | collective-permute-start | bytes 49160 | tf_op jit(solution)/shard_map/while/body/eval_jaxpr/ppermute | solution.py:22
  406.2 9.8 %collective-permute-start.1 = (f32[1,16,256]{2,1,0:T(8,128)S(1)}, f32[1,16,256]{2,1,0:T(8,128)S(1)}, u32[]{:S(2)}, u32[]{:S(2)}) collective-permute-start(f32[1,16,256]{2,1,0:T(8,128)S(1)} %get-tuple-element.140), channel_id=1, source_target_pairs={{0,4},{4,8},{8,12},{12,16},{16,20},{20,24},{24,28},{28,32},{32,36}... | collective-permute-start | bytes 49160 | tf_op jit(solution)/shard_map/while/body/eval_jaxpr/ppermute | solution.py:19
  417.7 4.4 collective-permute-start.3
  422.2 10.9 %collective-permute-start.5 = (f32[1,16,256]{2,1,0:T(8,128)S(1)}, f32[1,16,256]{2,1,0:T(8,128)S(1)}, u32[]{:S(2)}, u32[]{:S(2)}) collective-permute-start(f32[1,16,256]{2,1,0:T(8,128)S(1)} %get-tuple-element.105), channel_id=1, source_target_pairs={{0,4},{4,8},{8,12},{12,16},{16,20},{20,24},{24,28},{28,32},{32,36}... | collective-permute-start | bytes 49160 | tf_op jit(solution)/shard_map/ppermute | solution.py:19
  431.2 8.4 %collective-permute-start.4 = (f32[1,16,256]{2,1,0:T(8,128)S(1)}, f32[1,16,256]{2,1,0:T(8,128)S(1)}, u32[]{:S(2)}, u32[]{:S(2)}) collective-permute-start(f32[1,16,256]{2,1,0:T(8,128)S(1)} %get-tuple-element.104), channel_id=1, source_target_pairs={{4,0},{8,4},{12,8},{16,12},{20,16},{24,20},{28,24},{32,28},{36,32}... | collective-permute-start | bytes 49160 | tf_op jit(solution)/shard_map/ppermute | solution.py:22
  439.6 5.3 collective-permute-start.6
  440.9 4.8 collective-permute-start.7
  447.1 15.3 %all-to-all-start = ((f32[4,4,4,16,256]{4,3,2,1,0:T(8,128)}), f32[4,4,4,16,256]{4,3,2,1,0:T(8,128)S(1)}, u32[]{:S(2)}, u32[]{:S(2)}) async-start(f32[4,4,4,16,256]{4,3,2,1,0:T(8,128)} %stack.35), calls=%async_computation | async-start | bytes 2097152 | tf_op jit(solution)/shard_map/all_to_all | solution.py:76
  (11 other events, 195.0 us)
Sparse Core Ops, SparseCore 0:
  157.2 47.6 all-reduce.4
